TPU v7x, 128 devices: a whole 4x4x4 slice. The times are simulated.
128 devices in a mesh: req: 64 (over z, x, y), kv: 2 (over core).
Axes of the slice: x: 4, y: 4, z: 4, core: 2. Of those that a mesh axis runs over, the one named last changes fastest.
Arguments:
- tokens: bfloat16 [1024, 1536], P('req'), may hold values from -6 to 6
- gain_attn: bfloat16 [1536], replicated, may hold values from 0.099609375 to 1.8984375
- w_query: bfloat16 [1536, 1536], P(None, 'kv'), may hold values from -0.15625 to 0.15625
- w_key: bfloat16 [1536, 256], P(None, 'kv'), may hold values from -0.15625 to 0.15625
- w_value: bfloat16 [1536, 256], P(None, 'kv'), may hold values from -0.15625 to 0.15625
- w_out: bfloat16 [1536, 1536], P('kv'), may hold values from -0.15625 to 0.15625
- cache_k: bfloat16 [4096, 128, 256], P('req', None, 'kv'), may hold values from -720 to 720
- cache_v: bfloat16 [4096, 128, 256], P('req', None, 'kv'), may hold values from -6 to 6
- page_table: int32 [1024, 4], P('req'), may hold values from 0 to 63, as said below
- lengths: int32 [1024], replicated, may hold values from 1 to 512, as said below
- new_owner: int32 [64], replicated, may hold values from 0 to 63, as said below
- gain_moe: bfloat16 [1536], replicated, may hold values from 0.099609375 to 1.8984375
- w_router: bfloat16 [1536, 32], replicated, may hold values from -0.15625 to 0.15625
- routes: int32 [1024, 4], P(('req', 'kv')), may hold values from 0 to 31, all different within a row; in each aligned block of 8 rows (0 to 7, 8 to 15, ...) at most 2 rows name the same one
- w_gate: bfloat16 [64, 1536, 384], P('req', None, 'kv'), may hold values from -0.15625 to 0.15625
- w_up: bfloat16 [64, 1536, 384], P('req', None, 'kv'), may hold values from -0.15625 to 0.15625
- w_down: bfloat16 [64, 1536, 384], P('req', None, 'kv'), may hold values from -0.21875 to 0.21875
Outputs:
- layer_out: bfloat16 [1024, 1536], P(('req', 'kv'))
Inputs may be any that keep to these rules, and one draw needn't show every extreme that they name: `lengths`: the last slot of each device (15, 31, ...) holds at most 256, and some last slot holds exactly 256; some length equals 512. `page_table`: the page indices of the 16 slots of one device are together a permutation of 0 to 63. `new_owner`: A permutation of the devices of req. `routes`: in each aligned block of 8 rows (the rows of one device) no expert is named by more than 2 rows.
All inputs are finite; a program needn't handle non-finite values.
Results may differ from a plain program's by a relative error of at most 0.015.
The roundings to bfloat16 on the way count: a program that leaves them out, or rounds other values in their place, can miss the bound.
Values may be sent and summed in bfloat16 or wider, within the bound.
A program may use at most 128 MiB of HBM per device.

v0:
```python
import jax
import jax.numpy as jnp
from jax import lax
from jax.sharding import PartitionSpec as P

MOVE_LEN = 256


def rms_scaled(values, gain_vec):
    wide = values.astype(jnp.float32)
    squares = jnp.mean(wide * wide, axis=-1, keepdims=True)
    return (wide * lax.rsqrt(squares + 1e-06) * gain_vec.astype(jnp.float32)).astype(jnp.bfloat16)


def cache_partial(queries, page_keys, page_values, live_len):
    inv_root = queries.shape[-1] ** (-0.5)
    scores = (
        jnp.einsum("rgd,rtd->rgt", queries, page_keys, preferred_element_type=jnp.float32)
        * inv_root
    )
    positions = lax.broadcasted_iota(jnp.int32, scores.shape, 2)
    live_mask = positions < live_len[:, None, None]
    scores = jnp.where(live_mask, scores, -1e30)
    top_score = jnp.max(scores, axis=-1)
    weights = jnp.where(live_mask, jnp.exp(scores - top_score[..., None]), 0.0)
    totals = jnp.sum(weights, axis=-1)
    accumulated = jnp.einsum(
        "rgt,rtd->rgd",
        weights.astype(jnp.bfloat16),
        page_values,
        preferred_element_type=jnp.float32,
    )
    return (accumulated, top_score, totals)


def finish_heads(accumulated, top_score, totals, queries, key_now, value_now):
    inv_root = queries.shape[-1] ** (-0.5)
    own_score = (
        jnp.einsum("rgd,rd->rg", queries, key_now, preferred_element_type=jnp.float32) * inv_root
    )
    joint_max = jnp.maximum(top_score, own_score)
    old_part = jnp.exp(top_score - joint_max)
    new_part = jnp.exp(own_score - joint_max)
    merged = (
        accumulated * old_part[..., None]
        + new_part[..., None] * value_now.astype(jnp.float32)[:, None, :]
    )
    result = merged / (totals * old_part + new_part)[..., None]
    return result.astype(jnp.bfloat16).reshape(queries.shape[0], -1)


def shards(
    tokens,
    gain_attn,
    w_query,
    w_key,
    w_value,
    w_out,
    cache_k,
    cache_v,
    page_table,
    lengths,
    new_owner,
    gain_moe,
    w_router,
    routes,
    w_gate,
    w_up,
    w_down,
):
    req_dev = tokens.shape[0]
    half_rows = req_dev // 2
    req_count = lax.axis_size("req")
    req_index = lax.axis_index("req")
    kv_index = lax.axis_index("kv")
    last_slot = req_dev - 1
    normed = rms_scaled(tokens, gain_attn)
    head_dim = w_key.shape[1]
    groups = w_query.shape[1] // head_dim
    queries = (
        jnp.dot(normed, w_query, preferred_element_type=jnp.float32)
        .astype(jnp.bfloat16)
        .reshape(req_dev, groups, head_dim)
    )
    key_now = jnp.dot(normed, w_key, preferred_element_type=jnp.float32).astype(jnp.bfloat16)
    value_now = jnp.dot(normed, w_value, preferred_element_type=jnp.float32).astype(jnp.bfloat16)
    own_len = lax.dynamic_slice_in_dim(lengths, req_index * req_dev, req_dev)
    page_keys = cache_k[page_table].reshape(req_dev, -1, head_dim)
    page_values = cache_v[page_table].reshape(req_dev, -1, head_dim)
    peer_ids = jnp.arange(req_count, dtype=jnp.int32)
    target = new_owner[req_index]
    source = jnp.sum(jnp.where(new_owner == req_index, peer_ids, 0))
    empty_bf = jnp.zeros((), jnp.bfloat16)
    chosen = (peer_ids == target)[:, None, None]
    outgoing_k = jnp.where(chosen, page_keys[last_slot, :MOVE_LEN][None], empty_bf)
    outgoing_v = jnp.where(chosen, page_values[last_slot, :MOVE_LEN][None], empty_bf)
    arrived_k, arrived_v = (
        lax.all_to_all(outgoing_k, "req", split_axis=0, concat_axis=0, tiled=True),
        lax.all_to_all(outgoing_v, "req", split_axis=0, concat_axis=0, tiled=True),
    )
    page_keys = page_keys.at[last_slot, :MOVE_LEN].set(arrived_k[source])
    page_values = page_values.at[last_slot, :MOVE_LEN].set(arrived_v[source])
    live_len = own_len.at[last_slot].set(lengths[source * req_dev + last_slot])
    accumulated, top_score, totals = cache_partial(queries, page_keys, page_values, live_len)
    attended = finish_heads(accumulated, top_score, totals, queries, key_now, value_now)
    head_terms = jnp.dot(attended, w_out, preferred_element_type=jnp.float32)
    head_total = lax.psum_scatter(head_terms, "kv", scatter_dimension=0, tiled=True)
    residual = lax.dynamic_slice_in_dim(tokens, kv_index * half_rows, half_rows, 0)
    middle = (residual.astype(jnp.float32) + head_total).astype(jnp.bfloat16)
    normed_two = rms_scaled(middle, gain_moe)
    logits = jnp.dot(normed_two, w_router, preferred_element_type=jnp.float32)
    route_weight = jax.nn.softmax(jnp.take_along_axis(logits, routes, axis=1), axis=-1)
    experts = req_count // 2
    topk = routes.shape[1]
    capacity = max(2, half_rows * topk // experts)
    flat_routes = routes.reshape(-1)
    onehot = (flat_routes[:, None] == jnp.arange(experts, dtype=jnp.int32)[None, :]).astype(
        jnp.int32
    )
    slot_rank = jnp.sum((jnp.cumsum(onehot, axis=0) - onehot) * onehot, axis=1)
    expert_of_peer = peer_ids // 2
    slot_ids = jnp.arange(capacity, dtype=jnp.int32)
    placement_map = (flat_routes[None, None, :] == expert_of_peer[:, None, None]) & (
        slot_rank[None, None, :] == slot_ids[None, :, None]
    )
    placement_map = placement_map.astype(jnp.float32).reshape(req_count, capacity, half_rows, topk)
    picked = jnp.sum(placement_map, axis=-1)
    blending = jnp.sum(placement_map * route_weight[None, None], axis=-1)
    outgoing = jnp.einsum(
        "pci,id->pcd", picked.astype(jnp.bfloat16), normed_two, preferred_element_type=jnp.float32
    ).astype(jnp.bfloat16)
    gate_half, up_half, down_half = (
        lax.all_gather(w_gate, "kv", axis=2, tiled=True),
        lax.all_gather(w_up, "kv", axis=2, tiled=True),
        lax.all_gather(w_down, "kv", axis=2, tiled=True),
    )
    received = lax.all_to_all(outgoing, "req", split_axis=0, concat_axis=0, tiled=True)
    senders, slot_count, feature_count = received.shape
    flat_rows = received.reshape(senders * slot_count, feature_count)
    gate_val = jnp.dot(flat_rows, gate_half[0], preferred_element_type=jnp.float32)
    up_val = jnp.dot(flat_rows, up_half[0], preferred_element_type=jnp.float32)
    hidden = (jax.nn.relu(gate_val) * up_val).astype(jnp.bfloat16)
    result = lax.dot_general(
        hidden, down_half[0], (((1,), (1,)), ((), ())), preferred_element_type=jnp.float32
    )
    returned = lax.all_to_all(
        result.reshape(senders, slot_count, feature_count),
        "req",
        split_axis=0,
        concat_axis=0,
        tiled=True,
    )
    mixed = jnp.einsum("pci,pcd->id", blending, returned, precision=lax.Precision.HIGHEST)
    return (middle.astype(jnp.float32) + mixed).astype(jnp.bfloat16)


def solution(mesh):
    return jax.shard_map(
        shards,
        mesh=mesh,
        in_specs=(
            P("req", None),
            P(),
            P(None, "kv"),
            P(None, "kv"),
            P(None, "kv"),
            P("kv", None),
            P("req", None, "kv"),
            P("req", None, "kv"),
            P("req", None),
            P(),
            P(),
            P(),
            P(),
            P(("req", "kv"), None),
            P("req", None, "kv"),
            P("req", None, "kv"),
            P("req", None, "kv"),
        ),
        out_specs=P(("req", "kv"), None),
        check_vma=False,
    )
```

profile of v0, /device:TPU:0, one launch (start us, length us, event | category | flops | bytes accessed | tf_op | source)
XLA Modules:
  0.0 236.1 jit_solution(13709867377025384650)
XLA Ops:
  6.5 1.4 dynamic_slice.21
  7.9 0.6 iota_compare_fusion.3
  8.6 0.7 compare_select_fusion.1
  9.5 3.7 %gather_fusion = bf16[64,128,128]{2,1,0:T(8,128)(2,1)} fusion(bf16[64,128,128]{2,1,0:T(8,128)(2,1)} %param.29, s32[1024]{0:T(1024)S(1)} %pad_clamp_fusion), kind=kCustom, calls=%fused_computation | custom fusion | bytes 4194560 | tf_op jit(solution)/shard_map/gather | solution.py:88
  13.2 3.8 %gather_fusion.1 = bf16[64,128,128]{2,1,0:T(8,128)(2,1)} fusion(bf16[64,128,128]{2,1,0:T(8,128)(2,1)} %param.30, s32[1024]{0:T(1024)S(1)} %pad_clamp_fusion), kind=kCustom, calls=%fused_computation.1 | custom fusion | bytes 4194560 | tf_op jit(solution)/shard_map/gather | solution.py:89
  17.0 0.9 slice_bitcast_fusion
  17.8 2.6 %broadcast_select_fusion.1 = (bf16[64,256,128]{2,1,0:T(8,128)(2,1)S(1)}, bf16[64,256,128]{2,1,0:T(8,128)(2,1)}) fusion(pred[64]{0:T(512)(128)(4,1)S(1)} %iota_compare_fusion.3, bf16[256,128]{1,0:T(8,128)(2,1)S(1)} %get-tuple-element.53, bf16[256,128]{1,0:T(8,128)(2,1)S(1)} %get-tuple-element.52), kind=kLoop, calls=%fused_computation.4 | loop fusion | flops 4194304 | bytes 8519744 | tf_op jit(solution)/shard_map/jit(_where)/select_n | solution.py:95
  20.4 63.5 %all_to_all.20 = bf16[64,256,128]{2,1,0:T(8,128)(2,1)} all-to-all(bf16[64,256,128]{2,1,0:T(8,128)(2,1)S(1)} %get-tuple-element.48), channel_id=1, replica_groups=mesh['req'=64,'kv'=2] {'req'}, dimensions={0} | all-to-all | bytes 8388608 | tf_op jit(solution)/shard_map/all_to_all | solution.py:98
  83.9 6.6 %all-to-all-start.1 = ((bf16[64,256,128]{2,1,0:T(8,128)(2,1)}), bf16[64,256,128]{2,1,0:T(8,128)(2,1)}, u32[]{:S(2)}, u32[]{:S(2)}) async-start(bf16[64,256,128]{2,1,0:T(8,128)(2,1)} %get-tuple-element.49), calls=%async_computation.1 | async-start | bytes 8388608 | tf_op jit(solution)/shard_map/all_to_all | solution.py:99
  90.6 0.6 fusion.54
  93.3 2.1 convolution_convert_fusion.1
  96.2 0.8 dynamic_slice.19
  96.9 0.8 constant_dynamic-update-slice_fusion
  98.4 1.5 dynamic-slice_dynamic-update-slice_fusion.1
  99.8 2.3 fusion.62
  102.4 38.8 %all-to-all-done.1 = bf16[64,256,128]{2,1,0:T(8,128)(2,1)} async-done(((bf16[64,256,128]{2,1,0:T(8,128)(2,1)}), bf16[64,256,128]{2,1,0:T(8,128)(2,1)}, u32[]{:S(2)}, u32[]{:S(2)}) %all-to-all-start.1) | async-done | bytes 4194336 | tf_op jit(solution)/shard_map/all_to_all | solution.py:99
  141.2 1.5 dynamic-slice_dynamic-update-slice_fusion
  142.7 2.0 fusion.20
  144.7 1.1 fusion.39
  145.9 0.7 all-gather.6.cloned.1.call-update
  146.6 0.7 all-gather.4.cloned.1.call-update
  148.9 5.7 %reduce-scatter.2.cloned.1.call-done = f32[8,1536]{1,0:T(8,128)} async-done(((f32[16,1536]{1,0:T(8,128)}), f32[8,1536]{1,0:T(8,128)}) %reduce-scatter.2.cloned.1.call-update) | async-done | bytes 49168 | tf_op jit(solution)/shard_map/reduce_scatter | solution.py:107
  154.6 0.9 fusion.34
  155.7 0.7 gather_fusion.2
  157.8 22.7 %all_to_all.21 = bf16[64,2,1536]{2,1,0:T(2,128)(2,1)S(1)} all-to-all(bf16[64,2,1536]{2,1,0:T(2,128)(2,1)S(1)} %copy.70), channel_id=1, replica_groups=mesh['req'=64,'kv'=2] {'req'}, dimensions={0} | all-to-all | bytes 786432 | tf_op jit(solution)/shard_map/all_to_all | solution.py:137
  180.7 1.8 fusion.4
  182.6 2.1 all-gather.4.cloned.1.call-done
  184.6 1.8 fusion.15
  186.5 13.0 %all-gather.8.cloned.1.call-done = bf16[1,1536,384]{1,2,0:T(8,128)(2,1)} async-done(((bf16[1,1536,192]{1,2,0:T(8,128)(2,1)}), bf16[1,1536,384]{1,2,0:T(8,128)(2,1)}) %all-gather.8.cloned.1.call-update) | async-done | bytes 1179664 | tf_op jit(solution)/shard_map/all_gather | solution.py:135
  199.4 1.6 fusion.2
  201.7 26.7 %all_to_all.22 = f32[64,2,1536]{2,1,0:T(2,128)S(1)} all-to-all(f32[64,2,1536]{2,1,0:T(2,128)S(1)} %copy.73), channel_id=1, replica_groups=mesh['req'=64,'kv'=2] {'req'}, dimensions={0} | all-to-all | bytes 1572864 | tf_op jit(solution)/shard_map/all_to_all | solution.py:146
  228.4 1.2 fusion.1
  (66 shorter events, 5.3 us)
Async XLA Ops:
  6.5 138.2 %copy-start = (bf16[768,1536]{1,0:T(8,128)(2,1)S(1)}, bf16[768,1536]{1,0:T(8,128)(2,1)}, u32[]{:S(2)}) copy-start(bf16[768,1536]{1,0:T(8,128)(2,1)} %param.28) | copy-start | bytes 7077892
  83.9 6.7 %copy-start.8 = (s32[64]{0:T(128)S(1)}, s32[64]{0:T(128)}, u32[]{:S(2)}) copy-start(s32[64]{0:T(128)} %param.33) | copy-start | bytes 772
  83.9 9.2 %copy-start.5 = (bf16[1536]{0:T(1024)(128)(2,1)S(1)}, bf16[1536]{0:T(1024)(128)(2,1)}, u32[]{:S(2)}) copy-start(bf16[1536]{0:T(1024)(128)(2,1)} %param.24) | copy-start | bytes 9220
  83.9 9.3 %copy-start.1 = (bf16[16,1536]{1,0:T(8,128)(2,1)S(1)}, bf16[16,1536]{1,0:T(8,128)(2,1)}, u32[]{:S(2)}) copy-start(bf16[16,1536]{1,0:T(8,128)(2,1)} %param.23) | copy-start | bytes 147460
  83.9 57.3 %all-to-all-start.1 = ((bf16[64,256,128]{2,1,0:T(8,128)(2,1)}), bf16[64,256,128]{2,1,0:T(8,128)(2,1)}, u32[]{:S(2)}, u32[]{:S(2)}) async-start(bf16[64,256,128]{2,1,0:T(8,128)(2,1)} %get-tuple-element.49), calls=%async_computation.1 | async-start | bytes 8388608 | tf_op jit(solution)/shard_map/all_to_all | solution.py:99
  90.5 7.3 %copy-start.2 = (bf16[1536,128]{1,0:T(8,128)(2,1)S(1)}, bf16[1536,128]{1,0:T(8,128)(2,1)}, u32[]{:S(2)}) copy-start(bf16[1536,128]{1,0:T(8,128)(2,1)} %param.26) | copy-start | bytes 1179652
  90.5 7.6 %copy-start.3 = (bf16[1536,128]{1,0:T(8,128)(2,1)S(1)}, bf16[1536,128]{1,0:T(8,128)(2,1)}, u32[]{:S(2)}) copy-start(bf16[1536,128]{1,0:T(8,128)(2,1)} %param.27) | copy-start | bytes 1179652
  90.5 64.1 %reduce-scatter.2.cloned.1.call-start = ((), (), s32[]{:S(2)}) async-start(), calls=%async_computation.5 | async-start | bytes 147456 | tf_op jit(solution)/shard_map/reduce_scatter | solution.py:107
  144.7 3.2 %copy-start.4 = (s32[8,4]{0,1:T(4,128)S(1)}, s32[8,4]{0,1:T(4,128)}, u32[]{:S(2)}) copy-start(s32[8,4]{0,1:T(4,128)} %param.36) | copy-start | bytes 388
  144.7 3.4 %copy-start.6 = (bf16[1536]{0:T(1024)(128)(2,1)S(1)}, bf16[1536]{0:T(1024)(128)(2,1)}, u32[]{:S(2)}) copy-start(bf16[1536]{0:T(1024)(128)(2,1)} %param.34) | copy-start | bytes 9220
  144.7 10.8 %copy-start.7 = (bf16[1536,32]{0,1:T(8,128)(2,1)S(1)}, bf16[1536,32]{0,1:T(8,128)(2,1)}, u32[]{:S(2)}) copy-start(bf16[1536,32]{0,1:T(8,128)(2,1)} %param.35) | copy-start | bytes 294916
  145.8 34.9 %all-gather.6.cloned.1.call-start = ((), (), s32[]{:S(2)}) async-start(), calls=%async_computation.7 | async-start | bytes 1769472 | tf_op jit(solution)/shard_map/all_gather | solution.py:134
  146.6 38.1 %all-gather.4.cloned.1.call-start = ((), (), s32[]{:S(2)}) async-start(), calls=%async_computation.6 | async-start | bytes 1769472 | tf_op jit(solution)/shard_map/all_gather | solution.py:133
  147.3 52.1 %all-gather.8.cloned.1.call-start = ((), (), s32[]{:S(2)}) async-start(), calls=%async_computation.8 | async-start | bytes 1769472 | tf_op jit(solution)/shard_map/all_gather | solution.py:135
Sparse Core Ops, SparseCore 0:
  145.9 8.5 reduce-scatter.1
  156.2 13.4 all-gather.5
  171.3 13.2 all-gather.3
  186.1 13.2 all-gather.7
where the time goes:
time: 237 us; the launch traced here: 236 us
  blocking collectives  113 us (48%)
  waiting for transfers between devices  61.4 us (26%)
  local copies, waits for them, and re-layouts  17.2 us (7%)
  between operations  16 us (7%)
  matrix products  15.1 us (6%)
  other arithmetic  6.77 us (3%)
  starting transfers between devices  6.72 us (3%)
    all_to_all x1, blocking collectives, shards(): lax.all_to_all(outgoing_k, 'req', split_axis=0, concat_axis=0, tiled=True)  63.5 us
    all_to_all x1, waiting for transfers between devices, shards(): lax.all_to_all(outgoing_v, 'req', split_axis=0, concat_axis=0, tiled=True)  38.8 us
    all_to_all x1, blocking collectives, shards(): lax.all_to_all(result.reshape(senders, slot_count, feature_count), 'req',...  26.7 us
    all_to_all x1, blocking collectives, shards(): lax.all_to_all(outgoing, 'req', split_axis=0, concat_axis=0, tiled=True)  22.7 us
    all_gather x1, waiting for transfers between devices, shards(): lax.all_gather(w_down, 'kv', axis=2, tiled=True)  13 us
    all_to_all x1, starting transfers between devices, shards(): lax.all_to_all(outgoing_v, 'req', split_axis=0, concat_axis=0, tiled=True)  6.56 us
    reduce_scatter x1, waiting for transfers between devices, shards(): lax.psum_scatter(head_terms, 'kv', scatter_dimension=0, tiled=True)  5.66 us
  transfers between devices with their start and end apart: 5, of which 4 were waited for; matrix products, arithmetic and copies ran while one was open for 7% of the time, Pallas kernels for 0%

commit v1 on v0

--- a/solution.py
+++ b/solution.py
@@ -132,7 +132,9 @@
     gate_half, up_half, down_half = (
         lax.all_gather(w_gate, "kv", axis=2, tiled=True),
         lax.all_gather(w_up, "kv", axis=2, tiled=True),
-        lax.all_gather(w_down, "kv", axis=2, tiled=True),
+        jnp.concatenate(
+            lax.all_to_all(jnp.stack([w_down] * lax.axis_size("kv")), "kv", 0, 0), axis=2
+        ),
     )
     received = lax.all_to_all(outgoing, "req", split_axis=0, concat_axis=0, tiled=True)
     senders, slot_count, feature_count = received.shape

time: 237 us -> 227 us (0.958)
  blocking collectives: 113 us -> 84.9 us
  starting transfers between devices: 6.72 us -> 20.8 us
  local copies, waits for them, and re-layouts: 17.2 us -> 22 us
  waiting for transfers between devices: 61.4 us -> 57.7 us
    all_to_all x1 -> x0, blocking collectives: 22.7 us -> none  [shards(): lax.all_to_all(outgoing, 'req', split_axis=0, concat_axis=0, tiled=True)]
    all_to_all x0 -> x2, starting transfers between devices: none -> 14.1 us  [the longest x1 10.5 us: shards(): lax.all_to_all(outgoing, 'req', split_axis=0, concat_axis=0, tiled=True)]
    all_gather x1 -> x0, waiting for transfers between devices: 13 us -> none  [shards(): lax.all_gather(w_down, 'kv', axis=2, tiled=True)]
    all_to_all x0 -> x2, waiting for transfers between devices: none -> 11.3 us  [the longest x1 11.3 us: shards(): lax.all_to_all(outgoing, 'req', split_axis=0, concat_axis=0, tiled=True)]
    all_to_all x1, blocking collectives: 26.7 us -> 21.5 us  [shards(): lax.all_to_all(result.reshape(senders, slot_count, feature_count), 'req',...]
  transfers between devices with their start and end apart: 5 -> 6, of which waited for: 4 -> 3; matrix products, arithmetic and copies ran while one was open for 7% -> 11% of each run, Pallas kernels for 0% -> 0%
where the time goes in v1:
time: 227 us; the launch traced here: 225 us
  blocking collectives  84.9 us (37%)
  waiting for transfers between devices  57.7 us (25%)
  local copies, waits for them, and re-layouts  22 us (10%)
  starting transfers between devices  20.8 us (9%)
  matrix products  16.2 us (7%)
  between operations  16 us (7%)
  other arithmetic  7.88 us (3%)
    all_to_all x1, blocking collectives, shards(): lax.all_to_all(outgoing_k, 'req', split_axis=0, concat_axis=0, tiled=True)  63.5 us
    all_to_all x1, waiting for transfers between devices, shards(): lax.all_to_all(outgoing_v, 'req', split_axis=0, concat_axis=0, tiled=True)  38.8 us
    all_to_all x1, blocking collectives, shards(): lax.all_to_all(result.reshape(senders, slot_count, feature_count), 'req',...  21.5 us
    all_to_all x1, waiting for transfers between devices, shards(): lax.all_to_all(outgoing, 'req', split_axis=0, concat_axis=0, tiled=True)  11.3 us
    all_to_all x1, starting transfers between devices, shards(): lax.all_to_all(outgoing, 'req', split_axis=0, concat_axis=0, tiled=True)  10.5 us
    all_to_all x1, starting transfers between devices, shards(): lax.all_to_all(outgoing_v, 'req', split_axis=0, concat_axis=0, tiled=True)  6.56 us
    reduce_scatter x1, waiting for transfers between devices, shards(): lax.psum_scatter(head_terms, 'kv', scatter_dimension=0, tiled=True)  6.24 us
  transfers between devices with their start and end apart: 6, of which 3 were waited for; matrix products, arithmetic and copies ran while one was open for 11% of the time, Pallas kernels for 0%

profile of v1, /device:TPU:0, one launch (start us, length us, event | category | flops | bytes accessed | tf_op | source)
XLA Modules:
  0.0 225.5 jit_solution(10843557951506655670)
XLA Ops:
  6.5 1.4 dynamic_slice.21
  9.5 3.7 %gather_fusion = bf16[64,128,128]{2,1,0:T(8,128)(2,1)} fusion(bf16[64,128,128]{2,1,0:T(8,128)(2,1)} %param.29, s32[1024]{0:T(1024)S(1)} %pad_clamp_fusion), kind=kCustom, calls=%fused_computation | custom fusion | bytes 4194560 | tf_op jit(solution)/shard_map/gather | solution.py:88
  13.2 3.8 %gather_fusion.1 = bf16[64,128,128]{2,1,0:T(8,128)(2,1)} fusion(bf16[64,128,128]{2,1,0:T(8,128)(2,1)} %param.30, s32[1024]{0:T(1024)S(1)} %pad_clamp_fusion), kind=kCustom, calls=%fused_computation.1 | custom fusion | bytes 4194560 | tf_op jit(solution)/shard_map/gather | solution.py:89
  17.0 0.9 slice_bitcast_fusion
  17.8 2.6 %broadcast_select_fusion.1 = (bf16[64,256,128]{2,1,0:T(8,128)(2,1)S(1)}, bf16[64,256,128]{2,1,0:T(8,128)(2,1)}) fusion(pred[64]{0:T(512)(128)(4,1)S(1)} %iota_compare_fusion.3, bf16[256,128]{1,0:T(8,128)(2,1)S(1)} %get-tuple-element.53, bf16[256,128]{1,0:T(8,128)(2,1)S(1)} %get-tuple-element.52), kind=kLoop, calls=%fused_computation.4 | loop fusion | flops 4194304 | bytes 8519744 | tf_op jit(solution)/shard_map/jit(_where)/select_n | solution.py:95
  20.4 63.5 %all_to_all.25 = bf16[64,256,128]{2,1,0:T(8,128)(2,1)} all-to-all(bf16[64,256,128]{2,1,0:T(8,128)(2,1)S(1)} %get-tuple-element.48), channel_id=1, replica_groups=mesh['req'=64,'kv'=2] {'req'}, dimensions={0} | all-to-all | bytes 8388608 | tf_op jit(solution)/shard_map/all_to_all | solution.py:98
  83.9 6.6 %all-to-all-start.1 = ((bf16[64,256,128]{2,1,0:T(8,128)(2,1)}), bf16[64,256,128]{2,1,0:T(8,128)(2,1)}, u32[]{:S(2)}, u32[]{:S(2)}) async-start(bf16[64,256,128]{2,1,0:T(8,128)(2,1)} %get-tuple-element.49), calls=%async_computation.1 | async-start | bytes 8388608 | tf_op jit(solution)/shard_map/all_to_all | solution.py:99
  93.3 2.1 convolution_convert_fusion.1
  96.2 0.8 dynamic_slice.19
  96.9 0.8 constant_dynamic-update-slice_fusion
  98.4 1.5 dynamic-slice_dynamic-update-slice_fusion.1
  99.8 2.3 %fusion.61 = (f32[16,6]{1,0:T(8,128)S(1)}, f32[16,6,512]{2,1,0:T(8,128)S(1)}) fusion(bf16[16,6,128]{2,1,0:T(8,128)(2,1)S(1)} %reshape.249, bf16[16,512,128]{2,1,0:T(8,128)(2,1)} %dynamic-slice_dynamic-update-slice_fusion.1, s32[16]{0:T(128)S(1)} %constant_dynamic-update-slice_fusion), kind=kOutput, calls=%fused_computation.96 | convolution fusion | flops 12779424 | bytes 2318784 | tf_op jit(solution)/shard_map/rgd,rtd->rgt/dot_general | solution.py:18
  102.4 38.8 %all-to-all-done.1 = bf16[64,256,128]{2,1,0:T(8,128)(2,1)} async-done(((bf16[64,256,128]{2,1,0:T(8,128)(2,1)}), bf16[64,256,128]{2,1,0:T(8,128)(2,1)}, u32[]{:S(2)}, u32[]{:S(2)}) %all-to-all-start.1) | async-done | bytes 4194336 | tf_op jit(solution)/shard_map/all_to_all | solution.py:99
  141.2 1.5 dynamic-slice_dynamic-update-slice_fusion
  142.7 2.0 fusion.18
  144.7 1.0 fusion.38
  145.8 0.7 all-gather.5.cloned.1.call-update
  148.3 6.2 %reduce-scatter.2.cloned.1.call-done = f32[8,1536]{1,0:T(8,128)} async-done(((f32[16,1536]{1,0:T(8,128)}), f32[8,1536]{1,0:T(8,128)}) %reduce-scatter.2.cloned.1.call-update) | async-done | bytes 49168 | tf_op jit(solution)/shard_map/reduce_scatter | solution.py:107
  154.6 0.9 fusion.33
  157.4 1.1 copy.84
  158.5 10.5 %all-to-all-start.2 = ((bf16[64,2,1536]{2,1,0:T(2,128)(2,1)}), bf16[64,2,1536]{2,1,0:T(2,128)(2,1)S(1)}, u32[]{:S(2)}, u32[]{:S(2)}) async-start(bf16[64,2,1536]{2,1,0:T(2,128)(2,1)} %copy.84), calls=%async_computation.3 | async-start | bytes 786432 | tf_op jit(solution)/shard_map/all_to_all | solution.py:139
  169.1 1.1 pad_maximum_fusion
  170.2 11.3 %all-to-all-done.2 = bf16[64,2,1536]{2,1,0:T(2,128)(2,1)S(1)} async-done(((bf16[64,2,1536]{2,1,0:T(2,128)(2,1)}), bf16[64,2,1536]{2,1,0:T(2,128)(2,1)S(1)}, u32[]{:S(2)}, u32[]{:S(2)}) %all-to-all-start.2) | async-done | bytes 393248 | tf_op jit(solution)/shard_map/all_to_all | solution.py:139
  181.5 0.7 copy-done.1
  182.2 3.6 %all-to-all-start.3 = ((bf16[2,1,1536,192]{2,3,1,0:T(8,128)(2,1)}), bf16[2,1,1536,192]{2,3,1,0:T(8,128)(2,1)S(1)}, u32[]{:S(2)}, u32[]{:S(2)}) async-start(bf16[2,1,1536,192]{2,3,1,0:T(8,128)(2,1)} %pad_maximum_fusion), calls=%async_computation.4 | async-start | bytes 2359296 | tf_op jit(solution)/shard_map/all_to_all | solution.py:136
  185.8 1.9 reshape.254
  187.7 2.6 %fusion.2 = f32[128,384]{1,0:T(8,128)} fusion(bf16[128,1536]{1,0:T(8,128)(2,1)} %reshape.254, bf16[1,1536,384]{1,2,0:T(8,128)(2,1)} %all-gather.5.cloned.1.call-done), kind=kOutput, calls=%fused_computation.10 | convolution fusion | flops 150994944 | bytes 1769472 | tf_op jit(solution)/shard_map/dot_general | solution.py:143
  190.3 2.5 %fusion.13 = bf16[128,384]{1,0:T(8,128)(2,1)} fusion(f32[128,384]{1,0:T(8,128)} %fusion.2, bf16[128,1536]{1,0:T(8,128)(2,1)} %reshape.254, bf16[1,1536,384]{1,2,0:T(8,128)(2,1)} %all-gather.3.cloned.1.call-done), kind=kOutput, calls=%fused_computation.18 | convolution fusion | flops 151142400 | bytes 1867776 | tf_op jit(solution)/shard_map/dot_general | solution.py:142
  192.8 1.6 dot_general.52
  194.4 1.3 fusion.31
  196.3 21.5 %all_to_all.26 = f32[64,2,1536]{2,1,0:T(2,128)S(1)} all-to-all(f32[64,2,1536]{2,1,0:T(2,128)S(1)} %copy.88), channel_id=1, replica_groups=mesh['req'=64,'kv'=2] {'req'}, dimensions={0} | all-to-all | bytes 1572864 | tf_op jit(solution)/shard_map/all_to_all | solution.py:148
  217.8 1.2 fusion.1
  (75 shorter events, 7.5 us)
Async XLA Ops:
  6.5 138.2 %copy-start = (bf16[768,1536]{1,0:T(8,128)(2,1)S(1)}, bf16[768,1536]{1,0:T(8,128)(2,1)}, u32[]{:S(2)}) copy-start(bf16[768,1536]{1,0:T(8,128)(2,1)} %param.28) | copy-start | bytes 7077892
  83.9 6.7 %copy-start.12 = (s32[64]{0:T(128)S(1)}, s32[64]{0:T(128)}, u32[]{:S(2)}) copy-start(s32[64]{0:T(128)} %param.33) | copy-start | bytes 772
  83.9 9.2 %copy-start.9 = (bf16[1536]{0:T(1024)(128)(2,1)S(1)}, bf16[1536]{0:T(1024)(128)(2,1)}, u32[]{:S(2)}) copy-start(bf16[1536]{0:T(1024)(128)(2,1)} %param.24) | copy-start | bytes 9220
  83.9 9.3 %copy-start.2 = (bf16[16,1536]{1,0:T(8,128)(2,1)S(1)}, bf16[16,1536]{1,0:T(8,128)(2,1)}, u32[]{:S(2)}) copy-start(bf16[16,1536]{1,0:T(8,128)(2,1)} %param.23) | copy-start | bytes 147460
  83.9 57.3 %all-to-all-start.1 = ((bf16[64,256,128]{2,1,0:T(8,128)(2,1)}), bf16[64,256,128]{2,1,0:T(8,128)(2,1)}, u32[]{:S(2)}, u32[]{:S(2)}) async-start(bf16[64,256,128]{2,1,0:T(8,128)(2,1)} %get-tuple-element.49), calls=%async_computation.1 | async-start | bytes 8388608 | tf_op jit(solution)/shard_map/all_to_all | solution.py:99
  90.5 7.3 %copy-start.4 = (bf16[1536,128]{1,0:T(8,128)(2,1)S(1)}, bf16[1536,128]{1,0:T(8,128)(2,1)}, u32[]{:S(2)}) copy-start(bf16[1536,128]{1,0:T(8,128)(2,1)} %param.26) | copy-start | bytes 1179652
  90.5 7.6 %copy-start.5 = (bf16[1536,128]{1,0:T(8,128)(2,1)S(1)}, bf16[1536,128]{1,0:T(8,128)(2,1)}, u32[]{:S(2)}) copy-start(bf16[1536,128]{1,0:T(8,128)(2,1)} %param.27) | copy-start | bytes 1179652
  90.5 64.1 %reduce-scatter.2.cloned.1.call-start = ((), (), s32[]{:S(2)}) async-start(), calls=%async_computation.6 | async-start | bytes 147456 | tf_op jit(solution)/shard_map/reduce_scatter | solution.py:107
  144.7 2.6 %copy-start.8 = (s32[8,4]{0,1:T(4,128)S(1)}, s32[8,4]{0,1:T(4,128)}, u32[]{:S(2)}) copy-start(s32[8,4]{0,1:T(4,128)} %param.36) | copy-start | bytes 388
  144.7 2.8 %copy-start.10 = (bf16[1536]{0:T(1024)(128)(2,1)S(1)}, bf16[1536]{0:T(1024)(128)(2,1)}, u32[]{:S(2)}) copy-start(bf16[1536]{0:T(1024)(128)(2,1)} %param.34) | copy-start | bytes 9220
  144.7 10.8 %copy-start.11 = (bf16[1536,32]{0,1:T(8,128)(2,1)S(1)}, bf16[1536,32]{0,1:T(8,128)(2,1)}, u32[]{:S(2)}) copy-start(bf16[1536,32]{0,1:T(8,128)(2,1)} %param.35) | copy-start | bytes 294916
  145.8 41.9 %all-gather.5.cloned.1.call-start = ((), (), s32[]{:S(2)}) async-start(), calls=%async_computation.8 | async-start | bytes 1769472 | tf_op jit(solution)/shard_map/all_gather | solution.py:134
  146.6 43.7 %all-gather.3.cloned.1.call-start = ((), (), s32[]{:S(2)}) async-start(), calls=%async_computation.7 | async-start | bytes 1769472 | tf_op jit(solution)/shard_map/all_gather | solution.py:133
  155.5 1.6 copy-start.6
  155.7 13.4 %copy-start.3 = (bf16[1,1536,192]{1,2,0:T(8,128)(2,1)S(1)}, bf16[1,1536,192]{1,2,0:T(8,128)(2,1)}, u32[]{:S(2)}) copy-start(bf16[1,1536,192]{1,2,0:T(8,128)(2,1)} %param.39) | copy-start | bytes 1769476
  158.5 22.9 %all-to-all-start.2 = ((bf16[64,2,1536]{2,1,0:T(2,128)(2,1)}), bf16[64,2,1536]{2,1,0:T(2,128)(2,1)S(1)}, u32[]{:S(2)}, u32[]{:S(2)}) async-start(bf16[64,2,1536]{2,1,0:T(2,128)(2,1)} %copy.84), calls=%async_computation.3 | async-start | bytes 786432 | tf_op jit(solution)/shard_map/all_to_all | solution.py:139
  181.5 0.7 copy-start.1
  182.2 12.2 %all-to-all-start.3 = ((bf16[2,1,1536,192]{2,3,1,0:T(8,128)(2,1)}), bf16[2,1,1536,192]{2,3,1,0:T(8,128)(2,1)S(1)}, u32[]{:S(2)}, u32[]{:S(2)}) async-start(bf16[2,1,1536,192]{2,3,1,0:T(8,128)(2,1)} %pad_maximum_fusion), calls=%async_computation.4 | async-start | bytes 2359296 | tf_op jit(solution)/shard_map/all_to_all | solution.py:136
  194.4 23.4 %copy-start.7 = (bf16[8,1536]{1,0:T(8,128)(2,1)S(1)}, bf16[8,1536]{1,0:T(8,128)(2,1)}, u32[]{:S(2)}) copy-start(bf16[8,1536]{1,0:T(8,128)(2,1)} %copy-done.6) | copy-start | bytes 73732
Sparse Core Ops, SparseCore 0:
  145.9 8.5 reduce-scatter.1
  156.2 13.4 all-gather.4
  171.3 13.2 all-gather.2
